TPU v7x, 32 devices: a whole 2x2x4 slice. The times are simulated.
32 devices in a mesh: facet: 8 (over y, x, core), chan: 4 (over z).
Axes of the slice: x: 2, y: 2, z: 4, core: 2. Of those that a mesh axis runs over, the one named last changes fastest.
Arguments:
- model_taylor: float32 [2, 8, 2, 512, 512], P(None, 'facet'), may hold values from -6 to 6
- channel_offset: float32 [4], P('chan'), may hold values from -0.5 to 0.5
- assignment: int32 [8], replicated, may hold values from 0 to 7, each once
- observed: float32 [4, 8, 2, 4096], P('chan', 'facet'), may hold values from -12 to 12
- uv_bins: int32 [4, 8, 4096], P('chan', 'facet'), may hold values from 0 to 16383
- vis_counts: int32 [4, 8], P('chan', 'facet'), may hold values from 1 to 4096, 16384 in all within a row
Outputs:
- taylor_residual: float32 [2, 8, 2, 512, 512], P(None, 'facet', None, 'chan')
Inputs may be any that keep to these rules, and one draw needn't show every extreme that they name: A permutation: task t, held by helper t, works on subgrid assignment[t]. Slots 0 .. vis_counts - 1 of a task are live; the others are ignored.
All inputs are finite; a program needn't handle non-finite values. No bound on the sum of `vis_counts` on one device may be relied on, other than what follows from the above.
Results may differ from a plain program's by a relative error of at most 0.0003.
Values sent between devices are 32-bit elements; how exact they have to be, the bound alone decides.
A program may use at most 128 MiB of HBM per device.

v0:
```python
import functools

import jax
import jax.numpy as jnp
from jax import lax
from jax.experimental import pallas as pl
from jax.experimental.pallas import tpu as pltpu
from jax.sharding import PartitionSpec as P

XM = 128
FACET_COLS = 4
SUB_COLS = 4
IMAGE = 2048
TWO_PI = 6.283185307179586
F32 = jnp.float32
BF16 = jnp.bfloat16
MESH = pl.DeviceIdType.MESH
VMEM_SPEC = pl.BlockSpec(memory_space=pltpu.VMEM)
SMEM_SPEC = pl.BlockSpec(memory_space=pltpu.SMEM)
VMEM_LIMIT = 56 * 1024 * 1024


def cos_sin(turns):
    quarter = IMAGE // 4
    shift = quarter.bit_length() - 1
    step = (turns + quarter // 2) >> shift
    rest = turns - (step << shift)
    t = rest.astype(F32) * (TWO_PI / IMAGE)
    t2 = t * t
    s = t * (1.0 + t2 * (-1.0 / 6 + t2 * (1.0 / 120 + t2 * (-1.0 / 5040 + t2 * (1.0 / 362880)))))
    c = 1.0 + t2 * (-0.5 + t2 * (1.0 / 24 + t2 * (-1.0 / 720 + t2 * (1.0 / 40320))))
    odd = (step & 1) == 1
    cos = jnp.where(odd, s, c)
    sin = jnp.where(odd, c, s)
    cos = jnp.where(((step + 1) & 2) == 2, -cos, cos)
    sin = jnp.where((step & 2) == 2, -sin, sin)
    return cos, sin


def window(positions, length):
    cos, _ = cos_sin(((2 * positions + 1 - length) * (IMAGE // (2 * length))) & (IMAGE - 1))
    return (0.55 + 0.45 * cos) * (float(length) ** -0.5)


def phases(frequency, pixel):
    cos, sin = cos_sin((frequency * pixel) & (IMAGE - 1))
    return cos, -sin


def split(value):
    high = value.astype(BF16)
    return high, (value - high.astype(F32)).astype(BF16)


def put(high_ref, low_ref, where, value):
    high, low = split(value)
    high_ref[where] = high
    low_ref[where] = low


def dot3(a_high, a_low, b_high, b_low):
    dot = functools.partial(jnp.dot, preferred_element_type=F32)
    return dot(a_high, b_high) + (dot(a_low, b_high) + dot(a_high, b_low))


def iota(shape, dim):
    return lax.broadcasted_iota(jnp.int32, shape, dim)


def flipped(me, bit):
    size = 1 << bit
    return me + (1 - 2 * ((me // size) % 2)) * size


def flipped_all(me, mask):
    for bit in range(mask.bit_length()):
        if (mask >> bit) & 1:
            me = flipped(me, bit)
    return me


def build_forward(fs, row_pix, col_pix, halves, bh, bl, ah, al):
    cells = bh.shape[1] // 2
    total = ah.shape[0]
    chunk = 64

    @pl.loop(0, fs // chunk)
    def _(k):
        base = pl.multiple_of(k * chunk, chunk)
        y = base + iota((chunk, cells), 0)
        re, im = phases(iota((chunk, cells), 1), col_pix + y)
        w = window(base + iota((chunk, XM), 0), fs)[:, :1]
        re, im = re * w, im * w
        top, low = pl.ds(base, chunk), pl.ds(pl.multiple_of(fs + base, chunk), chunk)
        put(bh, bl, (top, slice(0, cells)), re)
        put(bh, bl, (top, slice(cells, 2 * cells)), im)
        put(bh, bl, (low, slice(0, cells)), -im)
        put(bh, bl, (low, slice(cells, 2 * cells)), re)

    @pl.loop(0, total // chunk)
    def _(k):
        base = pl.multiple_of(k * chunk, chunk)
        x = iota((chunk, fs), 1)
        re, im = phases(base + iota((chunk, fs), 0), row_pix + x)
        w = window(iota((8, fs), 1), fs)[:1]
        rows = pl.ds(base, chunk)
        put(ah, al, (rows, slice(0, fs)), re * w)
        put(ah, al, (rows, slice(fs, 2 * fs)), im * w)


def build_adjoint(fs, share, row_pix, col_pix, mz, bh, bl, ah, al):
    cells = bh.shape[0] // 2
    total = ah.shape[1] // 2
    chunk = 64

    @pl.loop(0, cells // chunk)
    def _(k):
        base = pl.multiple_of(k * chunk, chunk)
        re, im = phases(base + iota((chunk, fs), 0), col_pix + iota((chunk, fs), 1))
        w = window(iota((8, fs), 1), fs)[:1]
        re, im = re * w, im * w
        top, low = pl.ds(base, chunk), pl.ds(pl.multiple_of(cells + base, chunk), chunk)
        put(bh, bl, (top, slice(0, fs)), re)
        put(bh, bl, (top, slice(fs, 2 * fs)), -im)
        put(bh, bl, (low, slice(0, fs)), im)
        put(bh, bl, (low, slice(fs, 2 * fs)), re)

    x = mz * share + iota((share, total), 0)
    re, im = phases(iota((share, total), 1), row_pix + x)
    w = window(mz * share + iota((share, XM), 0), fs)[:, :1]
    put(ah, al, (slice(None), slice(0, total)), re * w)
    put(ah, al, (slice(None), slice(total, 2 * total)), im * w)


def image_rows(i, offset, fs, xb, mbuf, mh, ml, bh, bl, ph, plo):
    cells = bh.shape[1] // 2
    for p in range(2):
        value = mbuf[i, 0, p] + offset * mbuf[i, 1, p]
        put(mh, ml, (slice(None), slice(p * fs, (p + 1) * fs)), value)
    tile = 256
    top, low = slice(i * xb, (i + 1) * xb), slice(fs + i * xb, fs + (i + 1) * xb)
    for k in range(2 * cells // tile):
        cols = slice(k * tile, (k + 1) * tile)
        part = dot3(mh[...], ml[...], bh[:, cols], bl[:, cols])
        high, small = split(part)
        ph[top, cols] = high
        plo[top, cols] = small
        if k * tile < cells:
            other = slice(k * tile + cells, (k + 1) * tile + cells)
        else:
            other = slice(k * tile - cells, (k + 1) * tile - cells)
            high, small = -high, -small
        ph[low, other] = high
        plo[low, other] = small


def subgrid_plane(p, subs, ah, al, ph, plo, out):
    cells = ph.shape[1] // 2
    tile = 256
    for k in range(cells // tile):
        part = dot3(
            ah[...], al[...],
            ph[:, p * cells + k * tile:p * cells + (k + 1) * tile],
            plo[:, p * cells + k * tile:p * cells + (k + 1) * tile],
        )
        for a in range(subs // SUB_COLS):
            for b in range(tile // XM):
                s = a * SUB_COLS + k * (tile // XM) + b
                out[s, p] = part[a * XM:(a + 1) * XM, b * XM:(b + 1) * XM]


def misfit_blocks(count_ref, grid_ref, obs_ref, bins_ref, out_ref, lhs, acc):
    slots = bins_ref.shape[-1]
    parts, _, rows, _ = out_ref.shape
    for p in range(2):
        high, low = split(grid_ref[p].T)
        lhs[p * XM:(p + 1) * XM, :XM] = high
        lhs[p * XM:(p + 1) * XM, XM:] = low
    acc[...] = jnp.zeros_like(acc)
    count = count_ref[0, 0]
    chunk = 512

    @pl.loop(0, slots // chunk)
    def _(k):
        here = pl.ds(pl.multiple_of(k * chunk, chunk), chunk)
        bins = bins_ref[0, :, here]
        cell = iota((XM, chunk), 0)
        hot_u = jnp.where(cell == (bins >> 7), 1.0, 0.0).astype(BF16)
        at_v = cell == (bins & (XM - 1))
        picked = jnp.dot(lhs[...], jnp.concatenate([hot_u, hot_u], axis=0), preferred_element_type=F32)
        live = k * chunk + iota((1, chunk), 1) < count
        hot_v = jnp.where(at_v, 1.0, 0.0).astype(BF16)
        sides = []
        for p in range(2):
            predicted = jnp.sum(jnp.where(at_v, picked[p * XM:(p + 1) * XM], 0.0), axis=0, keepdims=True)
            misfit = jnp.where(live, obs_ref[0, 0, p:p + 1, here] - predicted, 0.0)
            high, low = split(misfit)
            sides.append(hot_v * high)
            sides.append(hot_v * low)
        acc[...] += lax.dot_general(
            hot_u, jnp.concatenate(sides, axis=0), (((1,), (1,)), ((), ())), preferred_element_type=F32
        )

    for p in range(2):
        value = acc[:, 2 * p * XM:(2 * p + 1) * XM] + acc[:, (2 * p + 1) * XM:(2 * p + 2) * XM]
        for q in range(parts):
            out_ref[q, p] = value[q * rows:(q + 1) * rows]


def adjoint_rows(subs, parts, slots, mz, in_ref, rh, rl):
    rows = in_ref.shape[-2]
    cells = SUB_COLS * XM
    total = rh.shape[0] // 2
    for s in range(subs):
        a, b = s // SUB_COLS, s % SUB_COLS
        for d in range(parts):
            q = (mz - d + parts) % parts
            top = pl.ds(pl.multiple_of(a * XM + q * rows, rows), rows)
            low = pl.ds(pl.multiple_of(total + a * XM + q * rows, rows), rows)
            for j in range(2):
                left = slice(2 * j * cells + b * XM, 2 * j * cells + (b + 1) * XM)
                right = slice((2 * j + 1) * cells + b * XM, (2 * j + 1) * cells + (b + 1) * XM)
                high, small = split(in_ref[slots[s], d, j, 0])
                rh[top, left] = high
                rl[top, left] = small
                rh[low, right] = -high
                rl[low, right] = -small
                high, small = split(in_ref[slots[s], d, j, 1])
                rh[top, right] = high
                rl[top, right] = small
                rh[low, left] = high
                rl[low, left] = small


def adjoint_images(share, fs, out_ref, bh, bl, ah, al, rh, rl, wh, wl):
    cells = SUB_COLS * XM
    tile = 256
    for k in range(4 * cells // tile):
        cols = slice(k * tile, (k + 1) * tile)
        part = dot3(ah[...], al[...], rh[:, cols], rl[:, cols])
        j, rest = k * tile // (2 * cells), k * tile % (2 * cells)
        put(wh, wl, (slice(j * share, (j + 1) * share), slice(rest, rest + tile)), part)
    for k in range(2 * fs // tile):
        cols = slice(k * tile, (k + 1) * tile)
        part = dot3(wh[...], wl[...], bh[:, cols], bl[:, cols])
        p, rest = k * tile // fs, k * tile % fs
        for j in range(2):
            out_ref[j, 0, p, :, rest:rest + tile] = part[j * share:(j + 1) * share]


def cycle_kernel(
    names, bits, parts, assign_ref, off_ref, count_ref, model_ref, obs_ref, bins_ref, out_ref, *scratch
):
    m = dict(zip(names, scratch))
    me, mz = lax.axis_index("facet"), lax.axis_index("chan")
    subs, fs, share = assign_ref.shape[0], model_ref.shape[-1], out_ref.shape[3]
    halves, xb = m["mbuf"].shape[0], m["mbuf"].shape[3]
    row_pix, col_pix = (me // FACET_COLS) * fs, (me % FACET_COLS) * fs

    loads = []
    for i in range(halves):
        load = pltpu.make_async_copy(
            model_ref.at[:, 0, :, pl.ds(i * xb, xb), :], m["mbuf"].at[i], m["load_sem"].at[i]
        )
        load.start()
        loads.append(load)
    barrier = pltpu.get_barrier_semaphore()
    for b in range(bits):
        pl.semaphore_signal(barrier, inc=1, device_id={"facet": flipped(me, b)}, device_id_type=MESH)
    for d in range(1, parts):
        pl.semaphore_signal(barrier, inc=1, device_id={"chan": (mz + d) % parts}, device_id_type=MESH)

    offset = off_ref[0]
    m["tile"][...] = jnp.full(m["tile"].shape, offset, F32)
    build_forward(fs, row_pix, col_pix, halves, m["bh"], m["bl"], m["ah"], m["al"])
    subgrid_of = [assign_ref[flipped_all(me, r)] for r in range(subs)]
    slots = []
    for s in range(subs):
        slot = jnp.int32(0)
        for r in range(1, subs):
            slot = jnp.where(subgrid_of[r] == s, r, slot)
        slots.append(slot)
    for i in range(halves):
        loads[i].wait()
        image_rows(i, offset, fs, xb, m["mbuf"], m["mh"], m["ml"], m["bh"], m["bl"], m["ph"], m["plo"])

    waits = []

    def chan_copy(src, dst, send, recv, d):
        copy = pltpu.make_async_remote_copy(
            src_ref=src, dst_ref=dst, send_sem=send.at[d - 1], recv_sem=recv.at[d - 1],
            device_id={"chan": (mz + d) % parts}, device_id_type=MESH,
        )
        copy.start()
        waits.append(copy)
        return copy

    orders = [[0] + list(range(1, bits)), [0] + list(range(bits - 1, 0, -1))]
    blk, acc, recv = m["blk"], m["acc"], m["recv"]
    source = {(r, p): blk for r in range(1 << bits) for p in range(2)}
    copies = {}

    def send(r, p, bit):
        copy = pltpu.make_async_remote_copy(
            src_ref=source[r, p].at[r, p],
            dst_ref=recv.at[r, p],
            send_sem=m["rs_send"].at[r, p],
            recv_sem=m["rs_recv"].at[r, p],
            device_id={"facet": flipped(me, bit)},
            device_id_type=MESH,
        )
        copy.start()
        copies[r, p] = copy
        waits.append(copy)

    def ranked(members, later):
        return sorted(members, key=lambda r: [-((r >> b) & 1) for b in later])

    for p in range(2):
        subgrid_plane(p, subs, m["ah"], m["al"], m["ph"], m["plo"], m["grids"])
        for r in range(subs):
            blk[r, p] = m["grids"][subgrid_of[r], p]
        if p == 0:
            pl.semaphore_wait(barrier, bits + parts - 1)
        for r in ranked([r for r in range(subs) if (r >> orders[p][0]) & 1], orders[p][1:]):
            send(r, p, orders[p][0])
    small = [chan_copy(m["tile"], m["offs"].at[d - 1], m["off_send"], m["off_recv"], d) for d in range(1, parts)]

    build_adjoint(fs, share, row_pix, col_pix, mz, m["cbh"], m["cbl"], m["cah"], m["cal"])

    members = [list(range(1 << bits)) for _ in range(2)]
    for i in range(bits):
        kept = []
        for p in range(2):
            bit = orders[p][i]
            members[p] = ranked([r for r in members[p] if not (r >> bit) & 1], orders[p][i + 1:])
            kept.append(members[p])
        for pair in zip(*kept):
            for p in range(2):
                r, bit = pair[p], orders[p][i]
                copies[r | (1 << bit), p].wait_recv()
                acc[r, p] = source[r, p][r, p] + recv[r | (1 << bit), p]
                source[r, p] = acc
                if i < bits - 1 and (r >> orders[p][i + 1]) & 1:
                    send(r, p, orders[p][i + 1])

    zsend, zrecv, offs, gbuf = m["zsend"], m["zrecv"], m["offs"], m["gbuf"]
    misfit_blocks(count_ref, acc.at[0], obs_ref, bins_ref, zsend, m["lhs"], m["macc"])

    first = [chan_copy(zsend.at[(mz + d) % parts], zrecv.at[d - 1], m["z_send"], m["z_recv"], d) for d in range(1, parts)]
    plain = zsend[mz]
    scaled = offset * plain
    for d in range(1, parts):
        small[d - 1].wait_recv()
        first[d - 1].wait_recv()
        block = zrecv[d - 1]
        plain += block
        scaled += offs[d - 1, :1, :] * block
    gbuf[0, 0, 0] = plain
    gbuf[0, 0, 1] = scaled

    spread_orders = [list(range(1, bits)) + [0], list(range(bits - 1, 0, -1)) + [0]]
    landed = {}

    def spread(d, j, r, start):
        for i in range(start, bits):
            bit = spread_orders[j][i]
            to = r | (1 << bit)
            copy = pltpu.make_async_remote_copy(
                src_ref=gbuf.at[r, d, j], dst_ref=gbuf.at[to, d, j],
                send_sem=m["ag_send"].at[d, j, to], recv_sem=m["ag_recv"].at[d, j, to],
                device_id={"facet": flipped(me, bit)}, device_id_type=MESH,
            )
            copy.start()
            landed[d, j, to] = copy
            waits.append(copy)

    second = [chan_copy(gbuf.at[0, 0], gbuf.at[0, d], m["t_send"], m["t_recv"], d) for d in range(1, parts)]
    for j in range(2):
        spread(0, j, 0, 0)
    for tau in range(1, parts + bits + 1):
        if tau < parts:
            second[tau - 1].wait_recv()
            for j in range(2):
                spread(tau, j, 0, 0)
        for i in range(bits):
            d = tau - 1 - i
            if not 0 <= d < parts:
                continue
            for k in range(1 << i):
                for j in range(2):
                    held = sum(1 << spread_orders[j][e] for e in range(i) if (k >> e) & 1)
                    r = held | (1 << spread_orders[j][i])
                    landed[d, j, r].wait_recv()
                    spread(d, j, r, i + 1)
    adjoint_rows(subs, parts, slots, mz, gbuf, m["rh"], m["rl"])
    adjoint_images(
        share, fs, out_ref, m["cbh"], m["cbl"], m["cah"], m["cal"], m["rh"], m["rl"], m["wh"], m["wl"]
    )
    for copy in waits:
        copy.wait_send()


def solution(mesh):
    facets, parts = mesh.shape["facet"], mesh.shape["chan"]
    bits = facets.bit_length() - 1

    def on_device(model_taylor, channel_offset, assignment, observed, uv_bins, vis_counts):
        subs, fs = assignment.shape[0], model_taylor.shape[-1]
        share, rows, halves = fs // parts, XM // parts, 2
        xb = fs // halves
        cells, total = SUB_COLS * XM, subs // SUB_COLS * XM
        vmem, dma = pltpu.VMEM, pltpu.SemaphoreType.DMA
        scratch = {
            "mbuf": vmem((halves, 2, 2, xb, fs), F32),
            "tile": vmem((8, XM), F32),
            "offs": vmem((parts - 1, 8, XM), F32),
            "grids": vmem((subs, 2, XM, XM), F32),
            "blk": vmem((subs, 2, XM, XM), F32),
            "acc": vmem((subs, 2, XM, XM), F32),
            "recv": vmem((subs, 2, XM, XM), F32),
            "lhs": vmem((2 * XM, 2 * XM), BF16),
            "macc": vmem((XM, 4 * XM), F32),
            "zsend": vmem((parts, 2, rows, XM), F32),
            "zrecv": vmem((parts - 1, 2, rows, XM), F32),
            "gbuf": vmem((facets, parts, 2, 2, rows, XM), F32),
        }
        for high, low, shape in (
            ("bh", "bl", (2 * fs, 2 * cells)),
            ("ah", "al", (total, 2 * fs)),
            ("mh", "ml", (xb, 2 * fs)),
            ("ph", "plo", (2 * fs, 2 * cells)),
            ("cbh", "cbl", (2 * cells, 2 * fs)),
            ("cah", "cal", (share, 2 * total)),
            ("rh", "rl", (2 * total, 4 * cells)),
            ("wh", "wl", (2 * share, 2 * cells)),
        ):
            scratch[high] = vmem(shape, BF16)
            scratch[low] = vmem(shape, BF16)
        scratch["load_sem"] = dma((halves,))
        scratch["rs_send"] = scratch["rs_recv"] = dma((facets, 2))
        for name in ("off", "z", "t"):
            scratch[name + "_send"] = scratch[name + "_recv"] = dma((parts - 1,))
        scratch["ag_send"] = scratch["ag_recv"] = dma((parts, 2, facets))
        return pl.pallas_call(
            functools.partial(cycle_kernel, list(scratch), bits, parts),
            out_shape=jax.ShapeDtypeStruct((2, 1, 2, share, fs), F32),
            in_specs=[SMEM_SPEC] * 3 + [pl.BlockSpec(memory_space=pl.ANY)] + [VMEM_SPEC] * 2,
            out_specs=VMEM_SPEC,
            scratch_shapes=list(scratch.values()),
            compiler_params=pltpu.CompilerParams(
                collective_id=0, has_side_effects=True, vmem_limit_bytes=VMEM_LIMIT
            ),
        )(assignment, channel_offset, vis_counts, model_taylor, observed, uv_bins)

    return jax.shard_map(
        on_device,
        mesh=mesh,
        in_specs=(
            P(None, "facet", None, None, None),
            P("chan"),
            P(),
            P("chan", "facet", None, None),
            P("chan", "facet", None),
            P("chan", "facet"),
        ),
        out_specs=P(None, "facet", None, "chan", None),
        check_vma=False,
    )
```

profile of v0, /device:TPU:1, one launch (start us, length us, event | category | flops | bytes accessed | tf_op | source)
XLA Modules:
  0.0 55.8 jit_solution(11433975229032713356)
XLA Ops:
  1.3 52.3 %shard_map.64 = f32[2,1,2,128,512]{4,3,2,1,0:T(8,128)} custom-call(s32[8]{0:T(128)} %assign_ref.1, f32[1]{0:T(128)S(6)} %copy.8.off_ref, s32[1,1]{1,0:T(1,128)S(6)} %copy.9.count_ref, f32[2,1,2,512,512]{4,3,2,1,0:T(8,128)} %model_ref.1, f32[1,1,2,4096]{3,2,1,0:T(2,128)} %obs_ref.1, s32[1,1,4096]{2,1,0:T(1,128)} %bins_ref.1), custom_call_target="tpu_custom_call" | custom-call | tf_op jit(solution)/shard_map/pallas_call | solution.py:445
  53.6 2.3 %copy.10 = f32[2,1,2,128,512]{4,3,2,1,0:T(8,128)} copy(f32[2,1,2,128,512]{4,3,2,1,0:T(8,128)} %shard_map.64) | data formatting | bytes 2097152
where the time goes:
time: 56.1 us; the launch traced here: 55.8 us
  Pallas kernels  52.3 us (93%)
  local copies, waits for them, and re-layouts  2.26 us (4%)
  between operations  1.3 us (2%)
    pallas_call x1, Pallas kernels, on_device(): pl.pallas_call(functools.partial(cycle_kernel, list(scratch), bits, parts...  52.3 us
    unnamed x1, local copies, waits for them, and re-layouts  2.26 us

commit v1 on v0

--- a/solution.py
+++ b/solution.py
@@ -169,67 +169,74 @@
                 out[s, p] = part[a * XM:(a + 1) * XM, b * XM:(b + 1) * XM]
 
 
-def misfit_blocks(count_ref, grid_ref, obs_ref, bins_ref, out_ref, lhs, acc):
+def build_hot(bins_ref, hot_u, hot_v):
+    slots = bins_ref.shape[-1]
+    chunk = 512
+
+    @pl.loop(0, slots // chunk)
+    def _(k):
+        here = pl.ds(pl.multiple_of(k * chunk, chunk), chunk)
+        bins = bins_ref[0, :, here]
+        cell = iota((XM, chunk), 0)
+        at_u = jnp.where(cell == (bins >> 7), 1.0, 0.0).astype(BF16)
+        hot_u[:XM, here] = at_u
+        hot_u[XM:, here] = at_u
+        hot_v[:, here] = jnp.where(cell == (bins & (XM - 1)), 1.0, 0.0).astype(BF16)
+
+
+def misfit_blocks(count_ref, grid_ref, obs_ref, bins_ref, out_ref, lhs, hot_u, hot_v, sides):
     slots = bins_ref.shape[-1]
     parts, _, rows, _ = out_ref.shape
     for p in range(2):
         high, low = split(grid_ref[p].T)
         lhs[p * XM:(p + 1) * XM, :XM] = high
         lhs[p * XM:(p + 1) * XM, XM:] = low
-    acc[...] = jnp.zeros_like(acc)
     count = count_ref[0, 0]
     chunk = 512
-
-    @pl.loop(0, slots // chunk)
-    def _(k):
-        here = pl.ds(pl.multiple_of(k * chunk, chunk), chunk)
-        bins = bins_ref[0, :, here]
-        cell = iota((XM, chunk), 0)
-        hot_u = jnp.where(cell == (bins >> 7), 1.0, 0.0).astype(BF16)
-        at_v = cell == (bins & (XM - 1))
-        picked = jnp.dot(lhs[...], jnp.concatenate([hot_u, hot_u], axis=0), preferred_element_type=F32)
+    for k in range(slots // chunk):
+        here = slice(k * chunk, (k + 1) * chunk)
+        at_v = iota((XM, chunk), 0) == (bins_ref[0, :, here] & (XM - 1))
+        picked = jnp.dot(lhs[...], hot_u[:, here], preferred_element_type=F32)
         live = k * chunk + iota((1, chunk), 1) < count
-        hot_v = jnp.where(at_v, 1.0, 0.0).astype(BF16)
-        sides = []
+        ones = hot_v[:, here]
         for p in range(2):
             predicted = jnp.sum(jnp.where(at_v, picked[p * XM:(p + 1) * XM], 0.0), axis=0, keepdims=True)
             misfit = jnp.where(live, obs_ref[0, 0, p:p + 1, here] - predicted, 0.0)
             high, low = split(misfit)
-            sides.append(hot_v * high)
-            sides.append(hot_v * low)
-        acc[...] += lax.dot_general(
-            hot_u, jnp.concatenate(sides, axis=0), (((1,), (1,)), ((), ())), preferred_element_type=F32
+            sides[2 * p * XM:(2 * p + 1) * XM, here] = ones * high
+            sides[(2 * p + 1) * XM:(2 * p + 2) * XM, here] = ones * low
+
+    for p in range(2):
+        both = lax.dot_general(
+            hot_u[:XM, :], sides[2 * p * XM:(2 * p + 2) * XM, :], (((1,), (1,)), ((), ())),
+            preferred_element_type=F32,
         )
-
-    for p in range(2):
-        value = acc[:, 2 * p * XM:(2 * p + 1) * XM] + acc[:, (2 * p + 1) * XM:(2 * p + 2) * XM]
+        value = both[:, :XM] + both[:, XM:]
         for q in range(parts):
             out_ref[q, p] = value[q * rows:(q + 1) * rows]
 
 
-def adjoint_rows(subs, parts, slots, mz, in_ref, rh, rl):
+def adjoint_rows(subs, slots, q, in_ref, rh, rl):
     rows = in_ref.shape[-2]
     cells = SUB_COLS * XM
     total = rh.shape[0] // 2
     for s in range(subs):
         a, b = s // SUB_COLS, s % SUB_COLS
-        for d in range(parts):
-            q = (mz - d + parts) % parts
-            top = pl.ds(pl.multiple_of(a * XM + q * rows, rows), rows)
-            low = pl.ds(pl.multiple_of(total + a * XM + q * rows, rows), rows)
-            for j in range(2):
-                left = slice(2 * j * cells + b * XM, 2 * j * cells + (b + 1) * XM)
-                right = slice((2 * j + 1) * cells + b * XM, (2 * j + 1) * cells + (b + 1) * XM)
-                high, small = split(in_ref[slots[s], d, j, 0])
-                rh[top, left] = high
-                rl[top, left] = small
-                rh[low, right] = -high
-                rl[low, right] = -small
-                high, small = split(in_ref[slots[s], d, j, 1])
-                rh[top, right] = high
-                rl[top, right] = small
-                rh[low, left] = high
-                rl[low, left] = small
+        top = pl.ds(pl.multiple_of(a * XM + q * rows, rows), rows)
+        low = pl.ds(pl.multiple_of(total + a * XM + q * rows, rows), rows)
+        for j in range(2):
+            left = slice(2 * j * cells + b * XM, 2 * j * cells + (b + 1) * XM)
+            right = slice((2 * j + 1) * cells + b * XM, (2 * j + 1) * cells + (b + 1) * XM)
+            high, small = split(in_ref[slots[s], j, 0])
+            rh[top, left] = high
+            rl[top, left] = small
+            rh[low, right] = -high
+            rl[low, right] = -small
+            high, small = split(in_ref[slots[s], j, 1])
+            rh[top, right] = high
+            rl[top, right] = small
+            rh[low, left] = high
+            rl[low, left] = small
 
 
 def adjoint_images(share, fs, out_ref, bh, bl, ah, al, rh, rl, wh, wl):
@@ -268,7 +275,7 @@
     for b in range(bits):
         pl.semaphore_signal(barrier, inc=1, device_id={"facet": flipped(me, b)}, device_id_type=MESH)
     for d in range(1, parts):
-        pl.semaphore_signal(barrier, inc=1, device_id={"chan": (mz + d) % parts}, device_id_type=MESH)
+        pl.semaphore_signal(barrier, inc=1, device_id={"chan": flipped_all(mz, d)}, device_id_type=MESH)
 
     offset = off_ref[0]
     m["tile"][...] = jnp.full(m["tile"].shape, offset, F32)
@@ -289,7 +296,7 @@
     def chan_copy(src, dst, send, recv, d):
         copy = pltpu.make_async_remote_copy(
             src_ref=src, dst_ref=dst, send_sem=send.at[d - 1], recv_sem=recv.at[d - 1],
-            device_id={"chan": (mz + d) % parts}, device_id_type=MESH,
+            device_id={"chan": flipped_all(mz, d)}, device_id_type=MESH,
         )
         copy.start()
         waits.append(copy)
@@ -327,6 +334,7 @@
     small = [chan_copy(m["tile"], m["offs"].at[d - 1], m["off_send"], m["off_recv"], d) for d in range(1, parts)]
 
     build_adjoint(fs, share, row_pix, col_pix, mz, m["cbh"], m["cbl"], m["cah"], m["cal"])
+    build_hot(bins_ref, m["hot_u"], m["hot_v"])
 
     members = [list(range(1 << bits)) for _ in range(2)]
     for i in range(bits):
@@ -344,10 +352,11 @@
                 if i < bits - 1 and (r >> orders[p][i + 1]) & 1:
                     send(r, p, orders[p][i + 1])
 
-    zsend, zrecv, offs, gbuf = m["zsend"], m["zrecv"], m["offs"], m["gbuf"]
-    misfit_blocks(count_ref, acc.at[0], obs_ref, bins_ref, zsend, m["lhs"], m["macc"])
-
-    first = [chan_copy(zsend.at[(mz + d) % parts], zrecv.at[d - 1], m["z_send"], m["z_recv"], d) for d in range(1, parts)]
+    zsend, zrecv, offs = m["zsend"], m["zrecv"], m["offs"]
+    gbufs = [m["gbuf%d" % d] for d in range(parts)]
+    misfit_blocks(count_ref, acc.at[0], obs_ref, bins_ref, zsend, m["lhs"], m["hot_u"], m["hot_v"], m["sides"])
+
+    first = [chan_copy(zsend.at[flipped_all(mz, d)], zrecv.at[d - 1], m["z_send"], m["z_recv"], d) for d in range(1, parts)]
     plain = zsend[mz]
     scaled = offset * plain
     for d in range(1, parts):
@@ -356,8 +365,8 @@
         block = zrecv[d - 1]
         plain += block
         scaled += offs[d - 1, :1, :] * block
-    gbuf[0, 0, 0] = plain
-    gbuf[0, 0, 1] = scaled
+    gbufs[0][0, 0] = plain
+    gbufs[0][0, 1] = scaled
 
     spread_orders = [list(range(1, bits)) + [0], list(range(bits - 1, 0, -1)) + [0]]
     landed = {}
@@ -367,7 +376,7 @@
             bit = spread_orders[j][i]
             to = r | (1 << bit)
             copy = pltpu.make_async_remote_copy(
-                src_ref=gbuf.at[r, d, j], dst_ref=gbuf.at[to, d, j],
+                src_ref=gbufs[d].at[r, j], dst_ref=gbufs[d].at[to, j],
                 send_sem=m["ag_send"].at[d, j, to], recv_sem=m["ag_recv"].at[d, j, to],
                 device_id={"facet": flipped(me, bit)}, device_id_type=MESH,
             )
@@ -375,7 +384,7 @@
             landed[d, j, to] = copy
             waits.append(copy)
 
-    second = [chan_copy(gbuf.at[0, 0], gbuf.at[0, d], m["t_send"], m["t_recv"], d) for d in range(1, parts)]
+    second = [chan_copy(gbufs[0].at[0], gbufs[d].at[0], m["t_send"], m["t_recv"], d) for d in range(1, parts)]
     for j in range(2):
         spread(0, j, 0, 0)
     for tau in range(1, parts + bits + 1):
@@ -393,7 +402,9 @@
                     r = held | (1 << spread_orders[j][i])
                     landed[d, j, r].wait_recv()
                     spread(d, j, r, i + 1)
-    adjoint_rows(subs, parts, slots, mz, gbuf, m["rh"], m["rl"])
+        done = tau - bits
+        if 0 <= done < parts:
+            adjoint_rows(subs, slots, flipped_all(mz, done), gbufs[done], m["rh"], m["rl"])
     adjoint_images(
         share, fs, out_ref, m["cbh"], m["cbl"], m["cah"], m["cal"], m["rh"], m["rl"], m["wh"], m["wl"]
     )
@@ -420,11 +431,14 @@
             "acc": vmem((subs, 2, XM, XM), F32),
             "recv": vmem((subs, 2, XM, XM), F32),
             "lhs": vmem((2 * XM, 2 * XM), BF16),
-            "macc": vmem((XM, 4 * XM), F32),
+            "hot_u": vmem((2 * XM, uv_bins.shape[-1]), BF16),
+            "hot_v": vmem((XM, uv_bins.shape[-1]), BF16),
+            "sides": vmem((4 * XM, uv_bins.shape[-1]), BF16),
             "zsend": vmem((parts, 2, rows, XM), F32),
             "zrecv": vmem((parts - 1, 2, rows, XM), F32),
-            "gbuf": vmem((facets, parts, 2, 2, rows, XM), F32),
         }
+        for d in range(parts):
+            scratch["gbuf%d" % d] = vmem((facets, 2, 2, rows, XM), F32)
         for high, low, shape in (
             ("bh", "bl", (2 * fs, 2 * cells)),
             ("ah", "al", (total, 2 * fs)),

time: 56.1 us -> 54.6 us (0.973)
  Pallas kernels: 52.3 us -> 50.8 us
    pallas_call x1, Pallas kernels: 52.3 us -> 50.8 us  [on_device(): pl.pallas_call(functools.partial(cycle_kernel, list(scratch), bits, parts...]
where the time goes in v1:
time: 54.6 us; the launch traced here: 54.3 us
  Pallas kernels  50.8 us (93%)
  local copies, waits for them, and re-layouts  2.26 us (4%)
  between operations  1.3 us (2%)
    pallas_call x1, Pallas kernels, on_device(): pl.pallas_call(functools.partial(cycle_kernel, list(scratch), bits, parts...  50.8 us
    unnamed x1, local copies, waits for them, and re-layouts  2.26 us

profile of v1, /device:TPU:1, one launch (start us, length us, event | category | flops | bytes accessed | tf_op | source)
XLA Modules:
  0.0 54.3 jit_solution(18292961350211967209)
XLA Ops:
  1.3 50.8 %shard_map.64 = f32[2,1,2,128,512]{4,3,2,1,0:T(8,128)} custom-call(s32[8]{0:T(128)} %assign_ref.1, f32[1]{0:T(128)S(6)} %copy.8.off_ref, s32[1,1]{1,0:T(1,128)S(6)} %copy.9.count_ref, f32[2,1,2,512,512]{4,3,2,1,0:T(8,128)} %model_ref.1, f32[1,1,2,4096]{3,2,1,0:T(2,128)} %obs_ref.1, s32[1,1,4096]{2,1,0:T(1,128)} %bins_ref.1), custom_call_target="tpu_custom_call" | custom-call | tf_op jit(solution)/shard_map/pallas_call | solution.py:459
  52.1 2.3 %copy.10 = f32[2,1,2,128,512]{4,3,2,1,0:T(8,128)} copy(f32[2,1,2,128,512]{4,3,2,1,0:T(8,128)} %shard_map.64) | data formatting | bytes 2097152

commit v2 on v1

--- a/solution.py
+++ b/solution.py
@@ -333,9 +333,6 @@
             send(r, p, orders[p][0])
     small = [chan_copy(m["tile"], m["offs"].at[d - 1], m["off_send"], m["off_recv"], d) for d in range(1, parts)]
 
-    build_adjoint(fs, share, row_pix, col_pix, mz, m["cbh"], m["cbl"], m["cah"], m["cal"])
-    build_hot(bins_ref, m["hot_u"], m["hot_v"])
-
     members = [list(range(1 << bits)) for _ in range(2)]
     for i in range(bits):
         kept = []
@@ -351,12 +348,15 @@
                 source[r, p] = acc
                 if i < bits - 1 and (r >> orders[p][i + 1]) & 1:
                     send(r, p, orders[p][i + 1])
+        if i == 0:
+            build_hot(bins_ref, m["hot_u"], m["hot_v"])
 
     zsend, zrecv, offs = m["zsend"], m["zrecv"], m["offs"]
     gbufs = [m["gbuf%d" % d] for d in range(parts)]
     misfit_blocks(count_ref, acc.at[0], obs_ref, bins_ref, zsend, m["lhs"], m["hot_u"], m["hot_v"], m["sides"])
 
     first = [chan_copy(zsend.at[flipped_all(mz, d)], zrecv.at[d - 1], m["z_send"], m["z_recv"], d) for d in range(1, parts)]
+    build_adjoint(fs, share, row_pix, col_pix, mz, m["cbh"], m["cbl"], m["cah"], m["cal"])
     plain = zsend[mz]
     scaled = offset * plain
     for d in range(1, parts):

time: 54.6 us -> 53 us (0.971)
  Pallas kernels: 50.8 us -> 49 us
    pallas_call x1, Pallas kernels: 50.8 us -> 49 us  [on_device(): pl.pallas_call(functools.partial(cycle_kernel, list(scratch), bits, parts...]
where the time goes in v2:
time: 53 us; the launch traced here: 52.5 us
  Pallas kernels  49 us (92%)
  local copies, waits for them, and re-layouts  2.26 us (4%)
  between operations  1.3 us (2%)
    pallas_call x1, Pallas kernels, on_device(): pl.pallas_call(functools.partial(cycle_kernel, list(scratch), bits, parts...  49 us
    unnamed x1, local copies, waits for them, and re-layouts  2.26 us

profile of v2, /device:TPU:1, one launch (start us, length us, event | category | flops | bytes accessed | tf_op | source)
XLA Modules:
  0.0 52.5 jit_solution(12693956073400420466)
XLA Ops:
  1.3 49.0 %shard_map.64 = f32[2,1,2,128,512]{4,3,2,1,0:T(8,128)} custom-call(s32[8]{0:T(128)} %assign_ref.1, f32[1]{0:T(128)S(6)} %copy.8.off_ref, s32[1,1]{1,0:T(1,128)S(6)} %copy.9.count_ref, f32[2,1,2,512,512]{4,3,2,1,0:T(8,128)} %model_ref.1, f32[1,1,2,4096]{3,2,1,0:T(2,128)} %obs_ref.1, s32[1,1,4096]{2,1,0:T(1,128)} %bins_ref.1), custom_call_target="tpu_custom_call" | custom-call | tf_op jit(solution)/shard_map/pallas_call | solution.py:459
  50.3 2.3 %copy.10 = f32[2,1,2,128,512]{4,3,2,1,0:T(8,128)} copy(f32[2,1,2,128,512]{4,3,2,1,0:T(8,128)} %shard_map.64) | data formatting | bytes 2097152
